TPU v7x, 128 devices: a whole 4x4x4 slice. The times are simulated.
128 devices in a mesh: row: 16 (over y, x_hi, core), col: 8 (over z, x_lo).
Axes of the slice: x: 4 (x_hi: 2, x_lo: 2; x = x_hi * 2 + x_lo), y: 4, z: 4, core: 2. Of those that a mesh axis runs over, the one named last changes fastest.
Arguments:
- features: float32 [8192, 256], P('row', 'col'), may hold values from -6 to 6
- weight: float32 [256, 256], replicated, may hold values from -0.375 to 0.375
- layer_bias: float32 [256], P('col'), may hold values from -3 to 3
- out_weight: float32 [2, 256], P(None, 'col'), may hold values from -0.375 to 0.375
- adj_tiles: float32 [16, 8, 4, 128, 128], P('row', 'col'), may hold values from -0.5 to 0.5
- tile_rows: int32 [16, 8, 4], P('row', 'col'), may hold values from 0 to 3
- tile_cols: int32 [16, 8, 4], P('row', 'col'), may hold values from 0 to 63, as said below
- tile_count: int32 [16, 8], P('row', 'col'), may hold values from 0 to 4, as said below
- port_rows: int32 [16, 128], P('row'), may hold values from 0 to 511
- targets: float32 [2, 2048], P(None, 'row'), may hold values from -6 to 6
Outputs:
- hidden: float32 [8192, 256], P('row', 'col')
- predictions: float32 [2, 2048], P(None, 'row')
- grad_weight: float32 [256, 256], P(None, 'col')
- grad_bias: float32 [256], P('col')
- grad_out_weight: float32 [2, 256], P(None, 'col')
Inputs may be any that keep to these rules, and one draw needn't show every extreme that they name: tile_cols[r, c, k] >= 4 r + tile_rows[r, c, k]; the live slots of all devices name distinct tile positions. The live slots of a device are its first tile_count slots; some device has all 4 slots live.
All inputs are finite; a program needn't handle non-finite values.
Results may differ from a plain program's by a relative error of at most 0.00017.
Values sent between devices are 32-bit elements; how exact they have to be, the bound alone decides.
No kernel may reach another device: no remote copies, remote signals or barrier semaphores. Data moves between devices by JAX's collectives and lax.ppermute only.
A program may use at most 64 MiB of HBM per device.

v0:
```python
import jax
import jax.numpy as jnp
from jax import lax
from jax.sharding import PartitionSpec as P


def per_device(
    features,
    weight,
    layer_bias,
    out_weight,
    adj_tiles,
    tile_rows,
    tile_cols,
    tile_count,
    port_rows,
    targets,
):
    row_devices = lax.axis_size("row")
    tile_data = adj_tiles[0, 0]
    local_tiles = tile_rows[0, 0]
    col_tiles = tile_cols[0, 0]
    slot_total = tile_data.shape[0]
    tile_edge = tile_data.shape[1]
    local_rows = features.shape[0]
    row_tiles = local_rows // tile_edge
    all_tiles = row_tiles * row_devices
    live_mask = (jnp.arange(slot_total, dtype=jnp.int32) < tile_count[0, 0]).astype(jnp.float32)
    masked = tile_data * live_mask[:, None, None]
    global_tiles = lax.axis_index("row") * row_tiles + local_tiles
    tile_index = jnp.arange(all_tiles, dtype=jnp.int32)[:, None]
    place_rows = (tile_index == global_tiles[None, :]).astype(jnp.float32)
    place_cols = (tile_index == col_tiles[None, :]).astype(jnp.float32)

    def aggregate(rows_full):
        feat_width = rows_full.shape[1]
        everything = lax.all_gather(rows_full, "row", axis=0, tiled=True)
        blocks = everything.reshape(all_tiles, tile_edge, feat_width)
        own_blocks = rows_full.reshape(row_tiles, tile_edge, feat_width)
        direct = jnp.einsum(
            "kab,kbf->kaf", masked, blocks[col_tiles], precision=lax.Precision.HIGHEST
        )
        mirror = jnp.einsum(
            "kab,kaf->kbf", masked, own_blocks[local_tiles], precision=lax.Precision.HIGHEST
        )
        result = jnp.einsum("nk,kaf->naf", place_rows, direct, precision=lax.Precision.HIGHEST)
        result = result + jnp.einsum(
            "nk,kaf->naf", place_cols, mirror, precision=lax.Precision.HIGHEST
        )
        summed = lax.psum_scatter(
            result.reshape(lax.axis_size("row") * local_rows, feat_width),
            "row",
            scatter_dimension=0,
            tiled=True,
        )
        return lax.psum_scatter(summed, "col", scatter_dimension=1, tiled=True)

    x_full = lax.all_gather(features, "col", axis=1, tiled=True)
    z_rows = jnp.dot(x_full, weight, precision=lax.Precision.HIGHEST)
    pre = aggregate(z_rows) + layer_bias[None, :]
    sigma = jax.nn.sigmoid(pre)
    hidden = pre * sigma
    port_index = port_rows[0]
    port_hidden = hidden[port_index]
    partial_pred = jnp.einsum("of,pf->op", out_weight, port_hidden, precision=lax.Precision.HIGHEST)
    predictions = lax.psum(partial_pred, "col")
    errors = predictions - targets
    grad_out_part = jnp.einsum("op,pf->of", errors, port_hidden, precision=lax.Precision.HIGHEST)
    port_grad = jnp.einsum("op,of->pf", errors, out_weight, precision=lax.Precision.HIGHEST)
    grad_hidden = jnp.zeros_like(hidden).at[port_index].add(port_grad)
    grad_pre = grad_hidden * (sigma * (1.0 + pre * (1.0 - sigma)))
    grad_full = lax.all_gather(grad_pre, "col", axis=1, tiled=True)
    back = aggregate(grad_full)
    grad_weight_part = jnp.dot(x_full.T, back, precision=lax.Precision.HIGHEST)
    grad_bias_part = jnp.sum(grad_pre, axis=0)
    grad_weight, grad_bias, grad_out_weight = lax.psum(
        (grad_weight_part, grad_bias_part, grad_out_part), "row"
    )
    return (hidden, predictions, grad_weight, grad_bias, grad_out_weight)


def solution(mesh):
    placed = (
        P("row", "col"),
        P(),
        P("col"),
        P(None, "col"),
        P("row", "col", None, None, None),
        P("row", "col", None),
        P("row", "col", None),
        P("row", "col"),
        P("row", None),
        P(None, "row"),
    )
    return jax.shard_map(
        per_device,
        mesh=mesh,
        in_specs=placed,
        out_specs=(P("row", "col"), P(None, "row"), P(None, "col"), P("col"), P(None, "col")),
        check_vma=False,
    )
```

profile of v0, /device:TPU:0, one launch (start us, length us, event | category | flops | bytes accessed | tf_op | source)
XLA Modules:
  0.0 642.7 jit_solution(13437956215964822083)
XLA Ops:
  7.2 31.8 %all_gather.12 = f32[512,256]{0,1:T(8,128)S(1)} all-gather(f32[512,32]{0,1:T(8,128)} %param.10), channel_id=1, replica_groups=mesh['row'=16,'col'=8] {'col'}, dimensions={1}, use_global_device_ids=true | all-gather | bytes 589824 | tf_op jit(solution)/shard_map/all_gather | solution.py:58
  39.0 1.8 fusion.36
  40.9 0.0 reduce-scatter.9.cloned.1.call-start
  41.6 0.7 fusion.29
  42.2 1.6 gather_fusion.1
  43.9 0.7 fusion.28
  44.5 0.7 add_bitcast_fusion
  45.2 1.7 fusion.9
  46.9 67.8 %all-gather.3.cloned.1.call-done = f32[8192,256]{1,0:T(8,128)} async-done(((f32[512,256]{1,0:T(8,128)}), f32[8192,256]{1,0:T(8,128)}) %all-gather.3.cloned.1.call-update) | async-done | bytes 8388624 | tf_op jit(solution)/shard_map/all_gather | solution.py:37
  114.6 4.0 gather_fusion
  118.6 1.6 fusion.10
  120.2 3.6 fusion.4
  123.8 3.9 convolution_add_fusion.1
  127.7 8.3 %copy.34 = f32[64,128,256]{2,1,0:T(8,128)} copy(f32[64,128,256]{2,0,1:T(8,128)S(1)} %convolution_add_fusion.1) | data formatting | bytes 16777216 | tf_op jit(solution)/shard_map/add | solution.py:47
  136.1 0.0 reduce-scatter.13.cloned.1.call-start
  136.1 100.2 %reduce-scatter.9.cloned.1.call-done = f32[512,256]{1,0:T(8,128)} async-done(((f32[8192,256]{1,0:T(8,128)}), f32[512,256]{1,0:T(8,128)}) %reduce-scatter.9.cloned.1.call-update) | async-done | bytes 524304 | tf_op jit(solution)/shard_map/reduce_scatter | solution.py:50
  236.3 2.0 copy.47
  238.4 0.0 all-gather.5.cloned.1.call-start
  238.5 37.5 %reduce-scatter.13.cloned.1.call-done = f32[32,512]{1,0:T(8,128)} async-done(((f32[256,512]{1,0:T(8,128)}), f32[32,512]{1,0:T(8,128)}) %reduce-scatter.13.cloned.1.call-update) | async-done | bytes 65552
  276.0 1.0 copy.48
  277.0 0.1 fusion.6
  277.1 0.6 gather_fusion.2
  277.7 0.2 convolution_bitcast_fusion.1
  277.9 16.6 %psum.28 = f32[2,128]{1,0:T(2,128)S(1)} all-reduce(f32[2,128]{1,0:T(2,128)S(1)} %convolution_bitcast_fusion.1), channel_id=1, replica_groups=mesh['row'=16,'col'=8] {'col'}, use_global_device_ids=true, to_apply=%region_2.0 | all-reduce | flops 256 | bytes 2048 | tf_op jit(solution)/shard_map/psum | solution.py:66
  294.5 0.3 fusion.33
  294.7 1.1 scatter_custom_fusion
  295.8 0.1 fusion.35
  296.0 0.1 copy.36
  296.1 31.4 %all_gather.14 = f32[512,256]{0,1:T(8,128)} all-gather(f32[512,32]{0,1:T(8,128)S(1)} %copy.36), channel_id=1, replica_groups=mesh['row'=16,'col'=8] {'col'}, dimensions={1}, use_global_device_ids=true | all-gather | bytes 589824 | tf_op jit(solution)/shard_map/all_gather | solution.py:72
  327.4 0.0 reduce-scatter.11.cloned.1.call-start
  327.5 1.2 copy.39
  328.7 0.6 gather_fusion.4
  329.3 0.7 fusion.7
  330.1 69.6 %all-gather.5.cloned.1.call-done = f32[8192,256]{0,1:T(8,128)} async-done(((f32[512,256]{0,1:T(8,128)}), f32[8192,256]{0,1:T(8,128)}) %all-gather.5.cloned.1.call-update) | async-done | bytes 8388624 | tf_op jit(solution)/shard_map/all_gather | solution.py:37
  399.7 9.0 %copy.37 = f32[8192,256]{1,0:T(8,128)} copy(f32[8192,256]{0,1:T(8,128)} %all-gather.5.cloned.1.call-done) | data formatting | bytes 16777216 | tf_op jit(solution)/shard_map/all_gather | solution.py:37
  408.6 4.0 gather_fusion.3
  412.6 0.6 fusion.8
  413.3 3.6 fusion.1
  416.8 3.9 convolution_add_fusion
  420.8 8.1 %copy.42 = f32[64,128,256]{2,1,0:T(8,128)} copy(f32[64,128,256]{2,0,1:T(8,128)S(1)} %convolution_add_fusion) | data formatting | bytes 16777216 | tf_op jit(solution)/shard_map/add | solution.py:47
  428.9 0.0 reduce-scatter.15.cloned.1.call-start
  428.9 100.2 %reduce-scatter.11.cloned.1.call-done = f32[512,256]{1,0:T(8,128)} async-done(((f32[8192,256]{1,0:T(8,128)}), f32[512,256]{1,0:T(8,128)}) %reduce-scatter.11.cloned.1.call-update) | async-done | bytes 524304 | tf_op jit(solution)/shard_map/reduce_scatter | solution.py:50
  529.2 2.0 copy.49
  531.2 0.7 copy.43
  532.0 0.2 fusion.31
  532.1 36.8 %reduce-scatter.15.cloned.1.call-done = f32[32,512]{1,0:T(8,128)} async-done(((f32[256,512]{1,0:T(8,128)}), f32[32,512]{1,0:T(8,128)}) %reduce-scatter.15.cloned.1.call-update) | async-done | bytes 65552
  568.9 1.4 convolution_bitcast_fusion
  570.3 65.6 %all-reduce = (f32[256,32]{0,1:T(8,128)}, f32[32]{0:T(128)}, f32[2,32]{1,0:T(2,128)}) all-reduce(f32[256,32]{0,1:T(8,128)S(1)} %convolution_bitcast_fusion, f32[32]{0:T(128)S(1)} %get-tuple-element.28, f32[2,32]{1,0:T(2,128)S(1)} %fusion.31), channel_id=1, replica_groups=mesh['row'=16,'col'=8] {'row'}, use_global_device_ids=true, to_apply=%region_6.0 | all-reduce | flops 8288 | bytes 66304 | tf_op jit(solution)/shard_map/psum | solution.py:76
  (30 shorter events, 0.2 us)
Async XLA Ops:
  7.2 31.8 %copy-start = (f32[256,256]{1,0:T(8,128)S(1)}, f32[256,256]{1,0:T(8,128)}, u32[]{:S(2)}) copy-start(f32[256,256]{1,0:T(8,128)} %param.11) | copy-start | bytes 786436
  7.2 116.6 %copy-start.6 = (s32[1,1,4]{2,1,0:T(1,128)S(1)}, s32[1,1,4]{2,1,0:T(1,128)}, u32[]{:S(2)}) copy-start(s32[1,1,4]{2,1,0:T(1,128)} %param.16) | copy-start | bytes 52
  7.2 107.5 %all-gather.3.cloned.1.call-start = ((), (), s32[]{:S(2)}) async-start(), calls=%async_computation.4 | async-start | bytes 8912896 | tf_op jit(solution)/shard_map/all_gather | solution.py:37
  40.9 195.5 %reduce-scatter.9.cloned.1.call-start = ((), (), s32[]{:S(2)}) async-start(), calls=%async_computation.5 | async-start | bytes 8912896 | tf_op jit(solution)/shard_map/reduce_scatter | solution.py:50
  136.0 102.4 %copy-start.8 = (s32[1,128]{1,0:T(1,128)S(1)}, s32[1,128]{1,0:T(1,128)}, u32[]{:S(2)}) copy-start(s32[1,128]{1,0:T(1,128)} %param.18) | copy-start | bytes 1540
  136.0 141.0 %copy-start.7 = (f32[32]{0:T(128)S(1)}, f32[32]{0:T(128)}, u32[]{:S(2)}) copy-start(f32[32]{0:T(128)} %param.12) | copy-start | bytes 388
  136.0 141.7 %copy-start.4 = (f32[2,32]{1,0:T(2,128)S(1)}, f32[2,32]{1,0:T(2,128)}, u32[]{:S(2)}) copy-start(f32[2,32]{1,0:T(2,128)} %param.13) | copy-start | bytes 772
  136.0 158.4 %copy-start.5 = (f32[2,128]{1,0:T(2,128)S(1)}, f32[2,128]{1,0:T(2,128)}, u32[]{:S(2)}) copy-start(f32[2,128]{1,0:T(2,128)} %param.19) | copy-start | bytes 3076
  136.0 193.3 %copy-start.2 = (f32[1,1,4,128,128]{4,3,2,1,0:T(8,128)S(1)}, f32[1,1,4,128,128]{4,3,2,1,0:T(8,128)}, u32[]{:S(2)}) copy-start(f32[1,1,4,128,128]{4,3,2,1,0:T(8,128)} %param.14) | copy-start | bytes 786436
  136.1 139.9 %reduce-scatter.13.cloned.1.call-start = ((), (), s32[]{:S(2)}) async-start(), calls=%async_computation.8 | async-start | bytes 589824
  238.4 161.3 %all-gather.5.cloned.1.call-start = ((), (), s32[]{:S(2)}) async-start(), calls=%async_computation.6 | async-start | bytes 8912896 | tf_op jit(solution)/shard_map/all_gather | solution.py:37
  294.5 237.5 %copy-start.3 = (f32[2,128]{1,0:T(2,128)}, f32[2,128]{1,0:T(2,128)S(1)}, u32[]{:S(2)}) copy-start(f32[2,128]{1,0:T(2,128)S(1)} %psum.28) | copy-start | bytes 3076
  327.4 201.7 %reduce-scatter.11.cloned.1.call-start = ((), (), s32[]{:S(2)}) async-start(), calls=%async_computation.7 | async-start | bytes 8912896 | tf_op jit(solution)/shard_map/reduce_scatter | solution.py:50
  420.8 215.1 %copy-start.1 = (f32[256,256]{1,0:T(8,128)S(1)}, f32[256,256]{1,0:T(8,128)}, u32[]{:S(2)}) copy-start(f32[256,256]{1,0:T(8,128)} %param.11) | copy-start | bytes 786436
  428.9 140.0 %reduce-scatter.15.cloned.1.call-start = ((), (), s32[]{:S(2)}) async-start(), calls=%async_computation.9 | async-start | bytes 589824
Sparse Core Ops, SparseCore 0:
  41.0 73.6 all-gather.2
  136.2 100.1 reduce-scatter.8
  238.7 37.2 reduce-scatter.12
  327.6 72.0 all-gather.4
  429.0 100.1 reduce-scatter.10
  531.5 37.3 reduce-scatter.14
where the time goes:
time: 644 us; the launch traced here: 643 us
  waiting for transfers between devices  412 us (64%)
  blocking collectives  145 us (23%)
  local copies, waits for them, and re-layouts  43.2 us (7%)
  matrix products  23.5 us (4%)
  between operations  15 us (2%)
    reduce_scatter x2, waiting for transfers between devices, aggregate(): lax.psum_scatter(result.reshape(lax.axis_size('row') * local_rows, feat_w...  200 us
    all_gather x2, waiting for transfers between devices, aggregate(): everything = lax.all_gather(rows_full, 'row', axis=0, tiled=True)  137 us
    unnamed x8, waiting for transfers between devices  74.4 us
    psum x1, blocking collectives, per_device(): lax.psum((grad_weight_part, grad_bias_part, grad_out_part), 'row')  65.6 us
    all_gather x1, blocking collectives, per_device(): x_full = lax.all_gather(features, 'col', axis=1, tiled=True)  31.8 us
    all_gather x1, blocking collectives, per_device(): grad_full = lax.all_gather(grad_pre, 'col', axis=1, tiled=True)  31.4 us
    psum x1, blocking collectives, per_device(): predictions = lax.psum(partial_pred, 'col')  16.6 us
    add x2, local copies, waits for them, and re-layouts, aggregate(): result + jnp.einsum('nk,kaf->naf', place_cols, mirror, precision=lax.Prec...  16.3 us
  transfers between devices with their start and end apart: 6, of which 6 were waited for; matrix products, arithmetic and copies ran while one was open for 1% of the time, Pallas kernels for 0%

commit v1 on v0

--- a/solution.py
+++ b/solution.py
@@ -69,7 +69,9 @@
     port_grad = jnp.einsum("op,of->pf", errors, out_weight, precision=lax.Precision.HIGHEST)
     grad_hidden = jnp.zeros_like(hidden).at[port_index].add(port_grad)
     grad_pre = grad_hidden * (sigma * (1.0 + pre * (1.0 - sigma)))
-    grad_full = lax.all_gather(grad_pre, "col", axis=1, tiled=True)
+    grad_full = jnp.concatenate(
+        lax.all_to_all(jnp.stack([grad_pre] * lax.axis_size("col")), "col", 0, 0), axis=1
+    )
     back = aggregate(grad_full)
     grad_weight_part = jnp.dot(x_full.T, back, precision=lax.Precision.HIGHEST)
     grad_bias_part = jnp.sum(grad_pre, axis=0)

time: 644 us -> 624 us (0.969)
  blocking collectives: 145 us -> 126 us
    all_gather x1 -> x0, blocking collectives: 31.4 us -> none  [per_device(): grad_full = lax.all_gather(grad_pre, 'col', axis=1, tiled=True)]
    all_to_all x0 -> x1, blocking collectives: none -> 11.8 us  [per_device(): lax.all_to_all(jnp.stack([grad_pre] * lax.axis_size('col')), 'col', 0, 0)]
where the time goes in v1:
time: 624 us; the launch traced here: 623 us
  waiting for transfers between devices  412 us (66%)
  blocking collectives  126 us (20%)
  local copies, waits for them, and re-layouts  43.5 us (7%)
  matrix products  23.5 us (4%)
  between operations  15 us (2%)
    reduce_scatter x2, waiting for transfers between devices, aggregate(): lax.psum_scatter(result.reshape(lax.axis_size('row') * local_rows, feat_w...  200 us
    all_gather x2, waiting for transfers between devices, aggregate(): everything = lax.all_gather(rows_full, 'row', axis=0, tiled=True)  137 us
    unnamed x8, waiting for transfers between devices  74.3 us
    psum x1, blocking collectives, per_device(): lax.psum((grad_weight_part, grad_bias_part, grad_out_part), 'row')  65.6 us
    all_gather x1, blocking collectives, per_device(): x_full = lax.all_gather(features, 'col', axis=1, tiled=True)  31.8 us
    psum x1, blocking collectives, per_device(): predictions = lax.psum(partial_pred, 'col')  16.6 us
    add x2, local copies, waits for them, and re-layouts, aggregate(): result + jnp.einsum('nk,kaf->naf', place_cols, mirror, precision=lax.Prec...  16.3 us
  transfers between devices with their start and end apart: 6, of which 6 were waited for; matrix products, arithmetic and copies ran while one was open for 1% of the time, Pallas kernels for 0%

profile of v1, /device:TPU:0, one launch (start us, length us, event | category | flops | bytes accessed | tf_op | source)
XLA Modules:
  0.0 623.2 jit_solution(8652503818630743323)
XLA Ops:
  7.2 31.8 %all_gather.9 = f32[512,256]{0,1:T(8,128)S(1)} all-gather(f32[512,32]{0,1:T(8,128)} %param.10), channel_id=1, replica_groups=mesh['row'=16,'col'=8] {'col'}, dimensions={1}, use_global_device_ids=true | all-gather | bytes 589824 | tf_op jit(solution)/shard_map/all_gather | solution.py:58
  39.0 1.8 fusion.36
  40.9 0.0 reduce-scatter.9.cloned.1.call-start
  41.6 0.7 fusion.29
  42.2 1.6 gather_fusion.1
  43.9 0.7 fusion.28
  44.5 0.7 add_bitcast_fusion
  45.2 1.7 fusion.9
  46.9 67.8 %all-gather.3.cloned.1.call-done = f32[8192,256]{1,0:T(8,128)} async-done(((f32[512,256]{1,0:T(8,128)}), f32[8192,256]{1,0:T(8,128)}) %all-gather.3.cloned.1.call-update) | async-done | bytes 8388624 | tf_op jit(solution)/shard_map/all_gather | solution.py:37
  114.6 4.0 gather_fusion
  118.6 1.6 fusion.10
  120.2 3.6 fusion.4
  123.8 3.9 convolution_add_fusion.1
  127.7 8.3 %copy.37 = f32[64,128,256]{2,1,0:T(8,128)} copy(f32[64,128,256]{2,0,1:T(8,128)S(1)} %convolution_add_fusion.1) | data formatting | bytes 16777216 | tf_op jit(solution)/shard_map/add | solution.py:47
  136.1 0.0 reduce-scatter.13.cloned.1.call-start
  136.1 100.2 %reduce-scatter.9.cloned.1.call-done = f32[512,256]{1,0:T(8,128)} async-done(((f32[8192,256]{1,0:T(8,128)}), f32[512,256]{1,0:T(8,128)}) %reduce-scatter.9.cloned.1.call-update) | async-done | bytes 524304 | tf_op jit(solution)/shard_map/reduce_scatter | solution.py:50
  236.3 2.0 copy.50
  238.5 37.5 %reduce-scatter.13.cloned.1.call-done = f32[32,512]{1,0:T(8,128)} async-done(((f32[256,512]{1,0:T(8,128)}), f32[32,512]{1,0:T(8,128)}) %reduce-scatter.13.cloned.1.call-update) | async-done | bytes 65552
  276.0 1.0 copy.51
  277.0 0.1 fusion.6
  277.1 0.6 gather_fusion.2
  277.7 0.2 convolution_bitcast_fusion.1
  277.9 16.6 %psum.28 = f32[2,128]{1,0:T(2,128)S(1)} all-reduce(f32[2,128]{1,0:T(2,128)S(1)} %convolution_bitcast_fusion.1), channel_id=1, replica_groups=mesh['row'=16,'col'=8] {'col'}, use_global_device_ids=true, to_apply=%region_2.0 | all-reduce | flops 256 | bytes 2048 | tf_op jit(solution)/shard_map/psum | solution.py:66
  294.5 0.3 fusion.33
  294.7 1.1 scatter_custom_fusion
  295.8 0.1 fusion.35
  296.0 0.1 copy.39
  296.1 0.1 stack.2
  296.1 11.8 %all_to_all.5 = f32[8,512,32]{1,2,0:T(8,128)} all-to-all(f32[8,512,32]{1,2,0:T(8,128)S(1)} %stack.2), channel_id=1, replica_groups=mesh['row'=16,'col'=8] {'col'}, dimensions={0} | all-to-all | bytes 1048576 | tf_op jit(solution)/shard_map/all_to_all | solution.py:73
  307.9 0.0 reduce-scatter.11.cloned.1.call-start
  308.0 1.2 reshape_reshape.3
  309.2 0.2 copy.42
  309.4 0.6 gather_fusion.4
  310.0 0.7 fusion.7
  310.7 69.4 %all-gather.5.cloned.1.call-done = f32[8192,256]{0,1:T(8,128)} async-done(((f32[512,256]{0,1:T(8,128)}), f32[8192,256]{0,1:T(8,128)}) %all-gather.5.cloned.1.call-update) | async-done | bytes 8388624 | tf_op jit(solution)/shard_map/all_gather | solution.py:37
  380.1 9.0 %copy.40 = f32[8192,256]{1,0:T(8,128)} copy(f32[8192,256]{0,1:T(8,128)} %all-gather.5.cloned.1.call-done) | data formatting | bytes 16777216 | tf_op jit(solution)/shard_map/all_gather | solution.py:37
  389.1 4.0 gather_fusion.3
  393.1 0.6 fusion.8
  393.7 3.6 fusion.1
  397.3 3.9 convolution_add_fusion
  401.3 8.1 %copy.45 = f32[64,128,256]{2,1,0:T(8,128)} copy(f32[64,128,256]{2,0,1:T(8,128)S(1)} %convolution_add_fusion) | data formatting | bytes 16777216 | tf_op jit(solution)/shard_map/add | solution.py:47
  409.4 100.3 %reduce-scatter.11.cloned.1.call-done = f32[512,256]{1,0:T(8,128)} async-done(((f32[8192,256]{1,0:T(8,128)}), f32[512,256]{1,0:T(8,128)}) %reduce-scatter.11.cloned.1.call-update) | async-done | bytes 524304 | tf_op jit(solution)/shard_map/reduce_scatter | solution.py:50
  509.7 2.0 copy.52
  511.7 0.7 copy.46
  512.5 0.2 fusion.31
  512.6 36.7 %reduce-scatter.15.cloned.1.call-done = f32[32,512]{1,0:T(8,128)} async-done(((f32[256,512]{1,0:T(8,128)}), f32[32,512]{1,0:T(8,128)}) %reduce-scatter.15.cloned.1.call-update) | async-done | bytes 65552
  549.3 1.4 convolution_bitcast_fusion
  550.7 65.6 %all-reduce = (f32[256,32]{0,1:T(8,128)}, f32[32]{0:T(128)}, f32[2,32]{1,0:T(2,128)}) all-reduce(f32[256,32]{0,1:T(8,128)S(1)} %convolution_bitcast_fusion, f32[32]{0:T(128)S(1)} %get-tuple-element.28, f32[2,32]{1,0:T(2,128)S(1)} %fusion.31), channel_id=1, replica_groups=mesh['row'=16,'col'=8] {'row'}, use_global_device_ids=true, to_apply=%region_6.0 | all-reduce | flops 8288 | bytes 66304 | tf_op jit(solution)/shard_map/psum | solution.py:78
  (32 shorter events, 0.3 us)
Async XLA Ops:
  7.2 31.8 %copy-start = (f32[256,256]{1,0:T(8,128)S(1)}, f32[256,256]{1,0:T(8,128)}, u32[]{:S(2)}) copy-start(f32[256,256]{1,0:T(8,128)} %param.11) | copy-start | bytes 786436
  7.2 116.6 %copy-start.6 = (s32[1,1,4]{2,1,0:T(1,128)S(1)}, s32[1,1,4]{2,1,0:T(1,128)}, u32[]{:S(2)}) copy-start(s32[1,1,4]{2,1,0:T(1,128)} %param.16) | copy-start | bytes 52
  7.2 107.5 %all-gather.3.cloned.1.call-start = ((), (), s32[]{:S(2)}) async-start(), calls=%async_computation.5 | async-start | bytes 8912896 | tf_op jit(solution)/shard_map/all_gather | solution.py:37
  40.9 195.5 %reduce-scatter.9.cloned.1.call-start = ((), (), s32[]{:S(2)}) async-start(), calls=%async_computation.6 | async-start | bytes 8912896 | tf_op jit(solution)/shard_map/reduce_scatter | solution.py:50
  136.0 102.4 %copy-start.8 = (s32[1,128]{1,0:T(1,128)S(1)}, s32[1,128]{1,0:T(1,128)}, u32[]{:S(2)}) copy-start(s32[1,128]{1,0:T(1,128)} %param.18) | copy-start | bytes 1540
  136.0 141.0 %copy-start.7 = (f32[32]{0:T(128)S(1)}, f32[32]{0:T(128)}, u32[]{:S(2)}) copy-start(f32[32]{0:T(128)} %param.12) | copy-start | bytes 388
  136.0 141.7 %copy-start.4 = (f32[2,32]{1,0:T(2,128)S(1)}, f32[2,32]{1,0:T(2,128)}, u32[]{:S(2)}) copy-start(f32[2,32]{1,0:T(2,128)} %param.13) | copy-start | bytes 772
  136.0 158.4 %copy-start.5 = (f32[2,128]{1,0:T(2,128)S(1)}, f32[2,128]{1,0:T(2,128)}, u32[]{:S(2)}) copy-start(f32[2,128]{1,0:T(2,128)} %param.19) | copy-start | bytes 3076
  136.0 174.0 %copy-start.2 = (f32[1,1,4,128,128]{4,3,2,1,0:T(8,128)S(1)}, f32[1,1,4,128,128]{4,3,2,1,0:T(8,128)}, u32[]{:S(2)}) copy-start(f32[1,1,4,128,128]{4,3,2,1,0:T(8,128)} %param.14) | copy-start | bytes 786436
  136.1 139.9 %reduce-scatter.13.cloned.1.call-start = ((), (), s32[]{:S(2)}) async-start(), calls=%async_computation.9 | async-start | bytes 589824
  238.4 141.8 %all-gather.5.cloned.1.call-start = ((), (), s32[]{:S(2)}) async-start(), calls=%async_computation.7 | async-start | bytes 8912896 | tf_op jit(solution)/shard_map/all_gather | solution.py:37
  294.5 218.0 %copy-start.3 = (f32[2,128]{1,0:T(2,128)}, f32[2,128]{1,0:T(2,128)S(1)}, u32[]{:S(2)}) copy-start(f32[2,128]{1,0:T(2,128)S(1)} %psum.28) | copy-start | bytes 3076
  307.9 201.8 %reduce-scatter.11.cloned.1.call-start = ((), (), s32[]{:S(2)}) async-start(), calls=%async_computation.8 | async-start | bytes 8912896 | tf_op jit(solution)/shard_map/reduce_scatter | solution.py:50
  401.3 215.1 %copy-start.1 = (f32[256,256]{1,0:T(8,128)S(1)}, f32[256,256]{1,0:T(8,128)}, u32[]{:S(2)}) copy-start(f32[256,256]{1,0:T(8,128)} %param.11) | copy-start | bytes 786436
  409.4 139.9 %reduce-scatter.15.cloned.1.call-start = ((), (), s32[]{:S(2)}) async-start(), calls=%async_computation.10 | async-start | bytes 589824
Sparse Core Ops, SparseCore 0:
  41.0 73.6 all-gather.2
  136.2 100.1 reduce-scatter.8
  238.7 37.2 reduce-scatter.12
  308.1 72.0 all-gather.4
  409.5 100.1 reduce-scatter.10
  512.0 37.2 reduce-scatter.14
